TPU v7x, 768 devices: a whole 4x8x12 slice. The times are simulated.
768 devices in a mesh: section: 24 (over x_lo, z), row: 8 (over y), col: 4 (over x_hi, core).
Axes of the slice: x: 4 (x_hi: 2, x_lo: 2; x = x_hi * 2 + x_lo), y: 8, z: 12, core: 2. Of those that a mesh axis runs over, the one named last changes fastest.
Arguments:
- upstream: bfloat16 [24, 6144, 512], P('section', ('row', 'col')), may hold values from -6 to 6
- attended: bfloat16 [24, 3072, 1024], P('section', 'col'), may hold values from -0.75 to 0.75
- weight: bfloat16 [24, 6144, 3072], P('section', 'row', 'col'), may hold values from -0.078125 to 0.078125
Outputs:
- attended_grad: bfloat16 [24, 3072, 1024], P('section', ('col', 'row'))
- weight_grad: bfloat16 [24, 6144, 3072], P('section', 'row', 'col')
All inputs are finite; a program needn't handle non-finite values.
Results may differ from a plain program's by a relative error of at most 0.001.
Values may be sent and summed in bfloat16 or wider, within the bound.
A program may use at most 32 MiB of HBM per device.

v0:
```python
import jax
import jax.numpy as jnp
from jax import lax
from jax.sharding import PartitionSpec as P


def passed_along(value, axis, steps):
    count = lax.axis_size(axis)
    pairs = [(source, (source + steps) % count) for source in range(count)]
    return lax.ppermute(value, axis, pairs)


def on_device(upstream, attended, weight):
    sections = lax.axis_size("section") // 2
    lower_half = lax.axis_index("section") < sections
    arrived = passed_along(upstream, "section", -1)[0]
    gathered = lax.all_gather(arrived, "col", axis=0, tiled=True)
    partner = passed_along(gathered, "section", sections)
    grad_panel = jnp.where(
        lower_half,
        jnp.concatenate([gathered, partner], axis=1),
        jnp.concatenate([partner, gathered], axis=1),
    )
    features = attended[0]
    weight_block = weight[0]
    weight_grad = jnp.einsum(
        "it,kt->ik", grad_panel, features, preferred_element_type=jnp.float32
    ).astype(jnp.bfloat16)
    share_rows = weight_block.shape[1] // lax.axis_size("row")
    partial_sum = jnp.einsum(
        "ik,it->kt", weight_block, grad_panel, preferred_element_type=jnp.float32
    )
    total = lax.psum(partial_sum, "row")
    summed = lax.dynamic_slice_in_dim(total, lax.axis_index("row") * share_rows, share_rows, 0)
    return (summed.astype(jnp.bfloat16)[None], weight_grad[None])


def solution(mesh):
    placed = (
        P("section", ("row", "col"), None),
        P("section", "col", None),
        P("section", "row", "col"),
    )
    return jax.shard_map(
        on_device,
        mesh=mesh,
        in_specs=placed,
        out_specs=(P("section", ("col", "row"), None), P("section", "row", "col")),
        check_vma=False,
    )
```

profile of v0, /device:TPU:16, one launch (start us, length us, event | category | flops | bytes accessed | tf_op | source)
XLA Modules:
  0.0 135.8 jit_solution(13503511506248388635)
XLA Ops:
  0.6 0.0 copy-start
  0.6 15.6 %collective-permute-start = (bf16[1,192,512]{2,1,0:T(8,128)(2,1)}, bf16[1,192,512]{2,1,0:T(8,128)(2,1)S(1)}, u32[]{:S(2)}, u32[]{:S(2)}) collective-permute-start(bf16[1,192,512]{2,1,0:T(8,128)(2,1)} %param.3), channel_id=1, source_target_pairs={{0,736},{32,0},{64,32},{96,64},{128,96},{160,128},{192,160},{224,1... | collective-permute-start | bytes 589832 | tf_op jit(solution)/shard_map/ppermute | solution.py:10
  16.3 4.5 %collective-permute-done = bf16[1,192,512]{2,1,0:T(8,128)(2,1)S(1)} collective-permute-done((bf16[1,192,512]{2,1,0:T(8,128)(2,1)}, bf16[1,192,512]{2,1,0:T(8,128)(2,1)S(1)}, u32[]{:S(2)}, u32[]{:S(2)}) %collective-permute-start) | collective-permute-done | bytes 196640 | tf_op jit(solution)/shard_map/ppermute | solution.py:10
  20.8 9.8 %all-gather = bf16[1,768,512]{2,1,0:T(8,128)(2,1)S(1)} all-gather(bf16[1,192,512]{2,1,0:T(8,128)(2,1)S(1)} %collective-permute-done), channel_id=2, replica_groups=mesh['section'=24,'row'=8,'col'=4] {'col'}, dimensions={1}, use_global_device_ids=true | all-gather | bytes 983040 | tf_op jit(solution)/shard_map/all_gather | solution.py:17
  30.6 0.0 copy-start.1
  30.6 2.1 %collective-permute-start.1 = (bf16[768,512]{1,0:T(8,128)(2,1)S(1)}, bf16[768,512]{1,0:T(8,128)(2,1)S(1)}, u32[]{:S(2)}, u32[]{:S(2)}) collective-permute-start(bf16[768,512]{1,0:T(8,128)(2,1)S(1)} %bitcast.17), channel_id=1, source_target_pairs={{0,384},{32,416},{64,448},{96,480},{128,512},{160,544},{192,576},{... | collective-permute-start | bytes 2359304 | tf_op jit(solution)/shard_map/ppermute | solution.py:10
  32.7 19.5 %collective-permute-done.1 = bf16[768,512]{1,0:T(8,128)(2,1)S(1)} collective-permute-done((bf16[768,512]{1,0:T(8,128)(2,1)S(1)}, bf16[768,512]{1,0:T(8,128)(2,1)S(1)}, u32[]{:S(2)}, u32[]{:S(2)}) %collective-permute-start.1) | collective-permute-done | bytes 786464 | tf_op jit(solution)/shard_map/ppermute | solution.py:10
  52.3 0.0 copy-done.1
  52.3 0.0 copy-start.2
  52.3 0.9 copy-done.2
  53.1 4.4 %convolution_bitcast_fusion = f32[768,1024]{0,1:T(8,128)} fusion(bf16[1,768,768]{2,1,0:T(8,128)(2,1)} %param.5, bf16[768,512]{1,0:T(8,128)(2,1)S(1)} %collective-permute-done.1, bf16[768,512]{1,0:T(8,128)(2,1)S(1)} %bitcast.18, pred[]{:T(512)S(6)} %lt.6), kind=kOutput, calls=%fused_computation | convolution fusion | flops 1215037440 | bytes 5898241 | tf_op jit(solution)/shard_map/ik,it->kt/dot_general | solution.py:30
  57.5 73.0 %all-reduce.1 = bf16[768,1024]{0,1:T(8,128)(2,1)S(1)} all-reduce(f32[768,1024]{0,1:T(8,128)} %convolution_bitcast_fusion), channel_id=1, replica_groups=mesh['section'=24,'row'=8,'col'=4] {'row'}, use_global_device_ids=true, to_apply=%region_0.1 | all-reduce | flops 786432 | bytes 4718592 | tf_op jit(solution)/shard_map/psum | solution.py:33
  130.5 0.1 fusion.9
  130.7 0.8 copy.5
  131.5 0.0 copy-done
  131.5 4.3 %fusion.5 = bf16[1,768,768]{2,1,0:T(8,128)(2,1)} fusion(bf16[1,768,1024]{2,1,0:T(8,128)(2,1)S(1)} %copy-done, bf16[768,512]{1,0:T(8,128)(2,1)} %copy-done.2, bf16[768,512]{1,0:T(8,128)(2,1)} %bitcast.19, pred[]{:T(512)S(6)} %lt.6), kind=kOutput, calls=%fused_computation.5 | convolution fusion | flops 1215627264 | bytes 4325377 | tf_op jit(solution)/shard_map/it,kt->ik/dot_general | solution.py:26
Async XLA Ops:
  0.6 130.9 %copy-start = (bf16[1,768,1024]{2,1,0:T(8,128)(2,1)S(1)}, bf16[1,768,1024]{2,1,0:T(8,128)(2,1)}, u32[]{:S(2)}) copy-start(bf16[1,768,1024]{2,1,0:T(8,128)(2,1)} %param.4) | copy-start | bytes 4718596
  0.6 20.1 %collective-permute-start = (bf16[1,192,512]{2,1,0:T(8,128)(2,1)}, bf16[1,192,512]{2,1,0:T(8,128)(2,1)S(1)}, u32[]{:S(2)}, u32[]{:S(2)}) collective-permute-start(bf16[1,192,512]{2,1,0:T(8,128)(2,1)} %param.3), channel_id=1, source_target_pairs={{0,736},{32,0},{64,32},{96,64},{128,96},{160,128},{192,160},{224,1... | collective-permute-start | bytes 589832 | tf_op jit(solution)/shard_map/ppermute | solution.py:10
  30.6 21.7 %copy-start.1 = (bf16[1,768,512]{2,1,0:T(8,128)(2,1)}, bf16[1,768,512]{2,1,0:T(8,128)(2,1)S(1)}, u32[]{:S(2)}) copy-start(bf16[1,768,512]{2,1,0:T(8,128)(2,1)S(1)} %all-gather) | copy-start | bytes 2359300
  30.6 21.7 %collective-permute-start.1 = (bf16[768,512]{1,0:T(8,128)(2,1)S(1)}, bf16[768,512]{1,0:T(8,128)(2,1)S(1)}, u32[]{:S(2)}, u32[]{:S(2)}) collective-permute-start(bf16[768,512]{1,0:T(8,128)(2,1)S(1)} %bitcast.17), channel_id=1, source_target_pairs={{0,384},{32,416},{64,448},{96,480},{128,512},{160,544},{192,576},{... | collective-permute-start | bytes 2359304 | tf_op jit(solution)/shard_map/ppermute | solution.py:10
  52.3 0.9 copy-start.2
where the time goes:
time: 136 us
  blocking collectives  82.9 us (61%)
  waiting for transfers between devices  24 us (18%)
  starting transfers between devices  17.8 us (13%)
  matrix products  8.69 us (6%)
  local copies, waits for them, and re-layouts  1.85 us (1%)
    psum x1, blocking collectives, on_device(): total = lax.psum(partial_sum, 'row')  73 us
    ppermute x2, waiting for transfers between devices, passed_along(): return lax.ppermute(value, axis, pairs)  24 us
    ppermute x2, starting transfers between devices, passed_along(): return lax.ppermute(value, axis, pairs)  17.8 us
    all_gather x1, blocking collectives, on_device(): gathered = lax.all_gather(arrived, 'col', axis=0, tiled=True)  9.82 us
    dot_general x1, matrix products, on_device(): jnp.einsum('ik,it->kt', weight_block, grad_panel, preferred_element_type=...  4.36 us
    dot_general x1, matrix products, on_device(): jnp.einsum('it,kt->ik', grad_panel, features, preferred_element_type=jnp....  4.33 us
  transfers between devices with their start and end apart: 2, of which 2 were waited for; matrix products, arithmetic and copies ran while one was open for 0% of the time, Pallas kernels for 0%

commit v1 on v0

v1 whole, which is shorter than its diff:
```python
import functools

import jax
import jax.numpy as jnp
from jax import lax
from jax.experimental import pallas as pl
from jax.experimental.pallas import tpu as pltpu
from jax.sharding import PartitionSpec as P

MESH = pl.DeviceIdType.MESH
CHUNKS = 4
ROWS = 8
OTHER = 4


def kernel(
    chips_z, up, attended, weight, ag_out, wg_out,
    panel, att, w, w_t, part, arrived, wg, ag,
    load_sem, store_sem, g_send, g_recv, r_send, r_recv,
):
    section, row, col = lax.axis_index("section"), lax.axis_index("row"), lax.axis_index("col")
    x_lo, z = section // chips_z, section % chips_z
    x_hi, core = col // 2, col % 2
    x = 2 * x_hi + x_lo
    width = panel.shape[-1]
    tokens = up.shape[-1]
    share = ag.shape[0]

    def at(x_pos, z_pos, core_pos, row_pos):
        return ((x_pos % 2) * chips_z + z_pos, row_pos, (x_pos // 2) * 2 + core_pos)

    z_before = (z + chips_z - 1) % chips_z
    z_after = (z + 1) % chips_z
    x_right, x_left, x_far = (x + 1) % 4, (x + 3) % 4, (x + 2) % 4
    below = at(x, z_before, core, row)
    above = at(x, z_after, core, row)
    right, left = at(x_right, z, core, row), at(x_left, z, core, row)
    sibling = at(x, z, 1 - core, row)
    up_row, down_row = at(x, z, core, (row + 1) % ROWS), at(x, z, core, (row + ROWS - 1) % ROWS)

    barrier = pltpu.get_barrier_semaphore()
    for other in (below, above, right, left, sibling, up_row, down_row):
        pl.semaphore_signal(barrier, inc=1, device_id=other, device_id_type=MESH)
    load_w = pltpu.make_async_copy(weight.at[0], w, load_sem.at[0])
    load_a = pltpu.make_async_copy(attended.at[0], att, load_sem.at[1])
    load_w.start()
    load_a.start()
    pl.semaphore_wait(barrier, 7)

    wrapped = (z + 1) // chips_z

    def slot(q, x_pos, core_pos):
        half = (x_pos % 2 + wrapped) % 2
        return panel.at[q, half, (x_pos // 2) * 2 + core_pos]

    def gather_copy(q, src, dst, send, recv, device):
        return pltpu.make_async_remote_copy(
            src_ref=src, dst_ref=dst, send_sem=g_send.at[q, send], recv_sem=g_recv.at[q, recv],
            device_id=device, device_id_type=MESH,
        )

    pending = []

    def send(q, src, dst, send_index, recv_index, device):
        copy = gather_copy(q, src, dst, send_index, recv_index, device)
        copy.start()
        pending.append(copy)

    sources = (x, x_left, x_right, x_far)

    def arrival(q, index):
        core_pos = core if index < OTHER else 1 - core
        place = slot(q, sources[index % OTHER], core_pos)
        gather_copy(q, place, place, 0, index, sibling).wait_recv()
        return place

    send_wrap = 1 - (z + chips_z - 1) // chips_z
    for q in range(CHUNKS):
        half = (x_lo + send_wrap) % 2
        send(q, up.at[0, :, pl.ds(q * width, width)], panel.at[q, half, col], 0, 0, below)

    load_w.wait()
    w_t[...] = w[...].T

    def own(q):
        place = arrival(q, 0)
        send(q, place, place, 1, 1, right)
        send(q, place, place, 2, 2, left)
        send(q, place, place, 3, OTHER, sibling)

    def near(q):
        from_left = arrival(q, 1)
        if q % 2 == 0:
            send(q, from_left, from_left, 7, 3, right)
        send(q, from_left, from_left, 4, OTHER + 1, sibling)
        from_right = arrival(q, 2)
        if q % 2 == 1:
            send(q, from_right, from_right, 7, 3, left)
        send(q, from_right, from_right, 5, OTHER + 2, sibling)

    def far(q):
        place = arrival(q, 3)
        send(q, place, place, 6, OTHER + 3, sibling)

    ways = (up_row, down_row)

    def ring_copy(q, way, half, step):
        ahead = OTHER - step
        dest = (row + (ahead if way == 0 else ROWS - ahead)) % ROWS
        return pltpu.make_async_remote_copy(
            src_ref=part.at[q, dest, half], dst_ref=arrived.at[q, way, step, half],
            send_sem=r_send.at[q, way, half, step], recv_sem=r_recv.at[q, way, half, step],
            device_id=ways[way], device_id_type=MESH,
        )

    def ring_send(q, way, half, step):
        copy = ring_copy(q, way, half, step)
        copy.start()
        pending.append(copy)

    def ring_start(q):
        for index in range(OTHER, 2 * OTHER):
            arrival(q, index)
        rows = panel.shape[2] * panel.shape[3]
        both = jnp.concatenate([panel[q, half].reshape(rows, width) for half in range(2)], axis=1)
        product = jnp.dot(w_t[...], both, preferred_element_type=jnp.float32)
        for half in range(2):
            part[q, :, half] = product[:, half * width:(half + 1) * width].reshape(ROWS, share, width)
        ring_send(q, 0, 0, 0)
        ring_send(q, 1, 1, 0)
        ring_send(q, 0, 1, 1)
        ring_send(q, 1, 0, 1)

    def ring_step(q, step):
        for half in range(2):
            for way in range(2):
                way = (way + half) % 2
                if step == 0 and way != half:
                    continue
                ring_copy(q, way, half, step).wait_recv()
                ahead = 3 - step
                dest = (row + (ahead if way == 0 else ROWS - ahead)) % ROWS
                if step < 3:
                    part[q, dest, half] += arrived[q, way, step, half]
                    ring_send(q, way, half, step + 1)
            if step == 3:
                total = part[q, row, half] + arrived[q, 0, 3, half] + arrived[q, 1, 3, half]
                begin = half * tokens + q * width
                ag[:, begin:begin + width] = total.astype(ag.dtype)

    stores = []

    def weight_grad(block):
        if block == 0:
            load_a.wait()
        lines = jnp.concatenate(
            [panel[q, half, block] for half in range(2) for q in range(CHUNKS)], axis=1
        )
        result = lax.dot_general(
            lines, att[...], (((1,), (1,)), ((), ())), preferred_element_type=jnp.float32
        )
        count = panel.shape[3]
        wg[pl.ds(block * count, count), :] = result.astype(wg.dtype)
        store = pltpu.make_async_copy(
            wg.at[pl.ds(block * count, count), :], wg_out.at[0, pl.ds(block * count, count), :],
            store_sem.at[block],
        )
        store.start()
        stores.append(store)

    own(0)
    own(1)
    near(0)
    own(2)
    far(0)
    near(1)
    own(3)
    ring_start(0)
    far(1)
    near(2)
    ring_start(1)
    far(2)
    near(3)
    ring_step(0, 0)
    ring_start(2)
    far(3)
    ring_step(1, 0)
    ring_start(3)
    ring_step(2, 0)
    weight_grad(0)
    ring_step(3, 0)
    ring_step(0, 1)
    weight_grad(1)
    ring_step(1, 1)
    ring_step(2, 1)
    weight_grad(2)
    ring_step(3, 1)
    ring_step(0, 2)
    weight_grad(3)
    for q in range(1, CHUNKS):
        ring_step(q, 2)
    for q in range(CHUNKS):
        ring_step(q, 3)
    store = pltpu.make_async_copy(ag, ag_out.at[0], store_sem.at[4])
    store.start()
    stores.append(store)
    for copy in pending:
        copy.wait_send()
    for store in stores:
        store.wait()


def on_device(chips_z, upstream, attended, weight):
    _, lines, tokens = upstream.shape
    _, features, all_tokens = attended.shape
    _, rows, _ = weight.shape
    share = features // ROWS
    width = tokens // CHUNKS
    bf16 = jnp.bfloat16
    dma = pltpu.SemaphoreType.DMA
    return pl.pallas_call(
        functools.partial(kernel, chips_z),
        out_shape=(
            jax.ShapeDtypeStruct((1, share, all_tokens), bf16),
            jax.ShapeDtypeStruct((1, rows, features), bf16),
        ),
        in_specs=[pl.BlockSpec(memory_space=pl.ANY)] * 3,
        out_specs=[pl.BlockSpec(memory_space=pl.ANY)] * 2,
        scratch_shapes=[
            pltpu.VMEM((CHUNKS, 2, rows // lines, lines, width), bf16),
            pltpu.VMEM((features, all_tokens), bf16),
            pltpu.VMEM((rows, features), bf16),
            pltpu.VMEM((features, rows), bf16),
            pltpu.VMEM((CHUNKS, ROWS, 2, share, width), jnp.float32),
            pltpu.VMEM((CHUNKS, 2, 4, 2, share, width), jnp.float32),
            pltpu.VMEM((rows, features), bf16),
            pltpu.VMEM((share, all_tokens), bf16),
            dma((2,)),
            dma((5,)),
            dma((CHUNKS, 8)),
            dma((CHUNKS, 8)),
            dma((CHUNKS, 2, 2, 4)),
            dma((CHUNKS, 2, 2, 4)),
        ],
        compiler_params=pltpu.CompilerParams(collective_id=0, has_side_effects=True),
    )(upstream, attended, weight)


def solution(mesh):
    placed = (
        P("section", ("row", "col"), None),
        P("section", "col", None),
        P("section", "row", "col"),
    )
    return jax.shard_map(
        functools.partial(on_device, mesh.shape["section"] // 2),
        mesh=mesh,
        in_specs=placed,
        out_specs=(P("section", ("col", "row"), None), P("section", "row", "col")),
        check_vma=False,
    )
```

time: 136 us -> 67.5 us (0.50)
  the two profiles are of different devices: /device:TPU:16 before, /device:TPU:1 now
where the time goes in v1:
time: 67.5 us; the launch traced here: 67.3 us
  Pallas kernels  62.7 us (93%)
  local copies, waits for them, and re-layouts  3.98 us (6%)
    pallas_call x1, Pallas kernels, on_device(): pl.pallas_call(functools.partial(kernel, chips_z), out_shape=(jax.ShapeDt...  62.7 us
    unnamed x2, local copies, waits for them, and re-layouts  3.98 us

profile of v1, /device:TPU:1, one launch (start us, length us, event | category | flops | bytes accessed | tf_op | source)
XLA Modules:
  0.0 67.3 jit_solution(7747089710851587222)
XLA Ops:
  0.6 62.7 %shard_map.50 = (bf16[1,96,1024]{2,1,0:T(8,128)(2,1)}, bf16[1,768,768]{2,1,0:T(8,128)(2,1)}) custom-call(bf16[1,192,512]{2,1,0:T(8,128)(2,1)} %up.1, bf16[1,768,1024]{2,1,0:T(8,128)(2,1)} %attended.1, bf16[1,768,768]{2,1,0:T(8,128)(2,1)} %weight.1), custom_call_target="tpu_custom_call" | custom-call | tf_op jit(solution)/shard_map/pallas_call | solution.py:221
  63.3 1.6 %copy.7 = bf16[1,96,1024]{2,1,0:T(8,128)(2,1)} copy(bf16[1,96,1024]{2,1,0:T(8,128)(2,1)} %get-tuple-element.4) | data formatting | bytes 393216
  64.9 2.4 %copy.8 = bf16[1,768,768]{2,1,0:T(8,128)(2,1)} copy(bf16[1,768,768]{2,1,0:T(8,128)(2,1)} %get-tuple-element.5) | data formatting | bytes 2359296

commit v2 on v0

v2 whole, which is shorter than its diff:
```python
import functools

import jax
import jax.numpy as jnp
from jax import lax
from jax.experimental import pallas as pl
from jax.experimental.pallas import tpu as pltpu
from jax.sharding import PartitionSpec as P

MESH = pl.DeviceIdType.MESH
CHUNKS = 4
ROWS = 8
OTHER = 4


def kernel(
    chips_z, up, attended, weight, ag, wg,
    panel, att, w, w_t, far_w, part, arrived,
    load_sem, w_send, w_recv, g_send, g_recv, r_send, r_recv,
):
    section, row, col = lax.axis_index("section"), lax.axis_index("row"), lax.axis_index("col")
    x_lo, z = section // chips_z, section % chips_z
    x_hi, core = col // 2, col % 2
    x = 2 * x_hi + x_lo
    width = panel.shape[-1]
    tokens = up.shape[-1]
    share, rows = w_t.shape[1:]

    def at(x_pos, z_pos, core_pos, row_pos):
        return ((x_pos % 2) * chips_z + z_pos, row_pos, (x_pos // 2) * 2 + core_pos)

    x_right, x_left, x_far = (x + 1) % 4, (x + 3) % 4, (x + 2) % 4
    below = at(x, (z + chips_z - 1) % chips_z, core, row)
    above = at(x, (z + 1) % chips_z, core, row)
    right, left = at(x_right, z, core, row), at(x_left, z, core, row)
    sibling = at(x, z, 1 - core, row)
    ways = at(x, z, core, (row + 1) % ROWS), at(x, z, core, (row + ROWS - 1) % ROWS)

    barrier = pltpu.get_barrier_semaphore()
    for other in (below, above, right, left, sibling, *ways):
        pl.semaphore_signal(barrier, inc=1, device_id=other, device_id_type=MESH)
    load_w = pltpu.make_async_copy(weight.at[0], w, load_sem.at[0])
    load_a = pltpu.make_async_copy(attended.at[0], att, load_sem.at[1])
    load_w.start()
    load_a.start()
    pl.semaphore_wait(barrier, 7)

    pending = []

    def remote(src, dst, send_sem, recv_sem, device):
        return pltpu.make_async_remote_copy(
            src_ref=src, dst_ref=dst, send_sem=send_sem, recv_sem=recv_sem,
            device_id=device, device_id_type=MESH,
        )

    def start(copy):
        copy.start()
        pending.append(copy)

    wrapped = (z + 1) // chips_z

    def slot(level, q, x_pos, core_pos):
        half = (x_pos % 2 + wrapped) % 2
        return panel.at[level, q, half, (x_pos // 2) * 2 + core_pos]

    def send(level, q, place, send_index, recv_index, device):
        start(remote(place, place, g_send.at[level, q, send_index], g_recv.at[level, q, recv_index], device))

    sources = (x, x_left, x_right, x_far)

    def arrival(level, q, index):
        place = slot(level, q, sources[index % OTHER], core if index < OTHER else 1 - core)
        remote(place, place, g_send.at[level, q, 0], g_recv.at[level, q, index], sibling).wait_recv()
        return place

    send_wrap = 1 - (z + chips_z - 1) // chips_z
    for q in range(CHUNKS):
        start(remote(
            up.at[0, :, pl.ds(q * width, width)], panel.at[0, q, (x_lo + send_wrap) % 2, col],
            g_send.at[0, q, 0], g_recv.at[0, q, 0], below,
        ))

    load_w.wait()
    w_t[...] = w[...].T.reshape(w_t.shape)

    def far_block(way):
        return remote(
            w_t.at[(row + OTHER) % ROWS], far_w.at[way], w_send.at[way], w_recv.at[way], ways[way]
        )

    for way in range(2):
        start(far_block(way))

    def own(q, level=0):
        place = arrival(level, q, 0)
        send(level, q, place, 1, 1, right)
        send(level, q, place, 2, 2, left)
        send(level, q, place, 3, OTHER, sibling)
        if level == 0:
            start(remote(
                place, slot(1, q, x, core), g_send.at[1, q, 0], g_recv.at[1, q, 0], ways[q % 2]
            ))

    def near(q, level=0):
        from_left = arrival(level, q, 1)
        if q % 2 == 0:
            send(level, q, from_left, 7, 3, right)
        send(level, q, from_left, 4, OTHER + 1, sibling)
        from_right = arrival(level, q, 2)
        if q % 2 == 1:
            send(level, q, from_right, 7, 3, left)
        send(level, q, from_right, 5, OTHER + 2, sibling)

    def far(q, level=0):
        place = arrival(level, q, 3)
        send(level, q, place, 6, OTHER + 3, sibling)

    def lines(level, q):
        for index in range(OTHER, 2 * OTHER):
            arrival(level, q, index)
        return jnp.concatenate([panel[level, q, half].reshape(rows, width) for half in range(2)], axis=1)

    def target(way, ahead):
        return (row + (ahead if way == 0 else ROWS - ahead)) % ROWS

    def ring_copy(q, way, half, step):
        return remote(
            part.at[q, target(way, 3 - step), half], arrived.at[q, way, step, half],
            r_send.at[q, way, half, step], r_recv.at[q, way, half, step], ways[way],
        )

    def ring_start(q):
        product = jnp.dot(
            w_t[...].reshape(ROWS * share, rows), lines(0, q), preferred_element_type=jnp.float32
        )
        for half in range(2):
            part[q, :, half] = product[:, half * width:(half + 1) * width].reshape(ROWS, share, width)
        for half in range(2):
            start(ring_copy(q, 1 - q % 2, half, 0))

    def lead_start(q):
        way = q % 2
        if q < 2:
            far_block(way).wait_recv()
        product = jnp.dot(far_w[way], lines(1, q), preferred_element_type=jnp.float32)
        for half in range(2):
            part[q, target(way, 3), half] += product[:, half * width:(half + 1) * width]
            start(ring_copy(q, way, half, 0))

    def ring_step(q, lead, step):
        way = q % 2 if lead else 1 - q % 2
        for half in range(2):
            ring_copy(q, way, half, step).wait_recv()
            if step < 2:
                part[q, target(way, 2 - step), half] += arrived[q, way, step, half]
                start(ring_copy(q, way, half, step + 1))
            elif lead:
                total = part[q, row, half] + arrived[q, 0, 2, half] + arrived[q, 1, 2, half]
                begin = half * tokens + q * width
                ag[0, :, begin:begin + width] = total.astype(ag.dtype)

    def weight_grad(block):
        if block == 0:
            load_a.wait()
        wide = jnp.concatenate(
            [panel[0, q, half, block] for half in range(2) for q in range(CHUNKS)], axis=1
        )
        result = lax.dot_general(
            wide, att[...], (((1,), (1,)), ((), ())), preferred_element_type=jnp.float32
        )
        count = panel.shape[-2]
        wg[0, pl.ds(block * count, count), :] = result.astype(wg.dtype)

    own(0)
    own(1)
    own(2)
    near(0)
    own(3)
    near(1)
    near(2)
    far(0)
    own(0, 1)
    own(1, 1)
    near(3)
    own(2, 1)
    own(3, 1)
    ring_start(0)
    far(1)
    far(2)
    ring_start(1)
    far(3)
    ring_start(2)
    ring_start(3)
    near(0, 1)
    near(1, 1)
    ring_step(0, False, 0)
    ring_step(1, False, 0)
    near(2, 1)
    near(3, 1)
    ring_step(2, False, 0)
    ring_step(3, False, 0)
    weight_grad(0)
    far(0, 1)
    far(1, 1)
    ring_step(0, False, 1)
    ring_step(1, False, 1)
    far(2, 1)
    far(3, 1)
    lead_start(0)
    lead_start(1)
    ring_step(2, False, 1)
    ring_step(3, False, 1)
    lead_start(2)
    lead_start(3)
    for q in range(CHUNKS):
        if q > 0:
            weight_grad(q)
        ring_step(q, False, 2)
    for step in range(3):
        for q in range(CHUNKS):
            ring_step(q, True, step)
    for copy in pending:
        copy.wait_send()


def on_device(chips_z, upstream, attended, weight):
    _, lines, tokens = upstream.shape
    _, features, all_tokens = attended.shape
    _, rows, _ = weight.shape
    share = features // ROWS
    width = tokens // CHUNKS
    bf16 = jnp.bfloat16
    dma = pltpu.SemaphoreType.DMA
    return pl.pallas_call(
        functools.partial(kernel, chips_z),
        out_shape=(
            pltpu.VMEM((1, share, all_tokens), bf16),
            pltpu.VMEM((1, rows, features), bf16),
        ),
        in_specs=[pl.BlockSpec(memory_space=pl.ANY)] * 3,
        out_specs=[pl.BlockSpec(memory_space=pltpu.VMEM)] * 2,
        scratch_shapes=[
            pltpu.VMEM((2, CHUNKS, 2, rows // lines, lines, width), bf16),
            pltpu.VMEM((features, all_tokens), bf16),
            pltpu.VMEM((rows, features), bf16),
            pltpu.VMEM((ROWS, share, rows), bf16),
            pltpu.VMEM((2, share, rows), bf16),
            pltpu.VMEM((CHUNKS, ROWS, 2, share, width), jnp.float32),
            pltpu.VMEM((CHUNKS, 2, 3, 2, share, width), jnp.float32),
            dma((2,)),
            dma((2,)),
            dma((2,)),
            dma((2, CHUNKS, 8)),
            dma((2, CHUNKS, 8)),
            dma((CHUNKS, 2, 2, 3)),
            dma((CHUNKS, 2, 2, 3)),
        ],
        compiler_params=pltpu.CompilerParams(collective_id=0, has_side_effects=True),
    )(upstream, attended, weight)


def solution(mesh):
    placed = (
        P("section", ("row", "col"), None),
        P("section", "col", None),
        P("section", "row", "col"),
    )
    return jax.shard_map(
        functools.partial(on_device, mesh.shape["section"] // 2),
        mesh=mesh,
        in_specs=placed,
        out_specs=(P("section", ("col", "row"), None), P("section", "row", "col")),
        check_vma=False,
    )
```

time: 136 us -> 61.2 us (0.45)
  the two profiles are of different devices: /device:TPU:16 before, /device:TPU:1 now
where the time goes in v2:
time: 61.2 us; the launch traced here: 60.6 us
  Pallas kernels  58.3 us (95%)
  local copies, waits for them, and re-layouts  1.69 us (3%)
  between operations  0.64 us (1%)
    pallas_call x1, Pallas kernels, on_device(): pl.pallas_call(functools.partial(kernel, chips_z), out_shape=(pltpu.VMEM(...  58.3 us
    unnamed x2, local copies, waits for them, and re-layouts  1.69 us

profile of v2, /device:TPU:1, one launch (start us, length us, event | category | flops | bytes accessed | tf_op | source)
XLA Modules:
  0.0 60.6 jit_solution(17436241458302337393)
XLA Ops:
  0.6 58.3 %shard_map.50 = (bf16[1,96,1024]{2,1,0:T(8,128)(2,1)S(1)}, bf16[1,768,768]{2,1,0:T(8,128)(2,1)S(1)}) custom-call(bf16[1,192,512]{2,1,0:T(8,128)(2,1)} %up.1, bf16[1,768,1024]{2,1,0:T(8,128)(2,1)} %attended.1, bf16[1,768,768]{2,1,0:T(8,128)(2,1)} %weight.1), custom_call_target="tpu_custom_call" | custom-call | tf_op jit(solution)/shard_map/pallas_call | solution.py:234
  59.0 0.7 %copy.7 = bf16[1,96,1024]{2,1,0:T(8,128)(2,1)} copy(bf16[1,96,1024]{2,1,0:T(8,128)(2,1)S(1)} %get-tuple-element.2) | data formatting | bytes 393216
  59.6 1.0 %copy.8 = bf16[1,768,768]{2,1,0:T(8,128)(2,1)} copy(bf16[1,768,768]{2,1,0:T(8,128)(2,1)S(1)} %get-tuple-element.3) | data formatting | bytes 2359296

commit v3 on v2

--- a/solution.py
+++ b/solution.py
@@ -10,6 +10,8 @@
 MESH = pl.DeviceIdType.MESH
 CHUNKS = 4
 ROWS = 8
+DIRECT = (0, 1, 2, 3)
+RELAY_LEFT = (1, 3)
 OTHER = 4
 
 
@@ -32,18 +34,20 @@
     x_right, x_left, x_far = (x + 1) % 4, (x + 3) % 4, (x + 2) % 4
     below = at(x, (z + chips_z - 1) % chips_z, core, row)
     above = at(x, (z + 1) % chips_z, core, row)
+    beyond = at(x_far, (z + chips_z - 1) % chips_z, core, row)
+    before = at(x_far, (z + 1) % chips_z, core, row)
     right, left = at(x_right, z, core, row), at(x_left, z, core, row)
     sibling = at(x, z, 1 - core, row)
     ways = at(x, z, core, (row + 1) % ROWS), at(x, z, core, (row + ROWS - 1) % ROWS)
 
     barrier = pltpu.get_barrier_semaphore()
-    for other in (below, above, right, left, sibling, *ways):
+    for other in (below, above, beyond, before, right, left, sibling, *ways):
         pl.semaphore_signal(barrier, inc=1, device_id=other, device_id_type=MESH)
     load_w = pltpu.make_async_copy(weight.at[0], w, load_sem.at[0])
     load_a = pltpu.make_async_copy(attended.at[0], att, load_sem.at[1])
     load_w.start()
     load_a.start()
-    pl.semaphore_wait(barrier, 7)
+    pl.semaphore_wait(barrier, 9)
 
     pending = []
 
@@ -75,10 +79,11 @@
 
     send_wrap = 1 - (z + chips_z - 1) // chips_z
     for q in range(CHUNKS):
-        start(remote(
-            up.at[0, :, pl.ds(q * width, width)], panel.at[0, q, (x_lo + send_wrap) % 2, col],
-            g_send.at[0, q, 0], g_recv.at[0, q, 0], below,
-        ))
+        chunk = up.at[0, :, pl.ds(q * width, width)]
+        place = panel.at[0, q, (x_lo + send_wrap) % 2, col]
+        start(remote(chunk, place, g_send.at[0, q, 0], g_recv.at[0, q, 0], below))
+        if q in DIRECT:
+            start(remote(chunk, place, g_send.at[0, q, 7], g_recv.at[0, q, 3], beyond))
 
     load_w.wait()
     w_t[...] = w[...].T.reshape(w_t.shape)
@@ -90,6 +95,9 @@
 
     for way in range(2):
         start(far_block(way))
+
+    half_here = (x_lo + wrapped) % 2
+    onward = at(x, z, core, (row + 1 + half_here * (ROWS - 2)) % ROWS)
 
     def own(q, level=0):
         place = arrival(level, q, 0)
@@ -98,16 +106,17 @@
         send(level, q, place, 3, OTHER, sibling)
         if level == 0:
             start(remote(
-                place, slot(1, q, x, core), g_send.at[1, q, 0], g_recv.at[1, q, 0], ways[q % 2]
+                place, slot(1, q, x, core), g_send.at[1, q, 0], g_recv.at[1, q, 0], onward
             ))
 
     def near(q, level=0):
         from_left = arrival(level, q, 1)
-        if q % 2 == 0:
+        relayed = level > 0 or q not in DIRECT
+        if relayed and q not in RELAY_LEFT:
             send(level, q, from_left, 7, 3, right)
         send(level, q, from_left, 4, OTHER + 1, sibling)
         from_right = arrival(level, q, 2)
-        if q % 2 == 1:
+        if relayed and q in RELAY_LEFT:
             send(level, q, from_right, 7, 3, left)
         send(level, q, from_right, 5, OTHER + 2, sibling)
 
@@ -136,20 +145,22 @@
         for half in range(2):
             part[q, :, half] = product[:, half * width:(half + 1) * width].reshape(ROWS, share, width)
         for half in range(2):
-            start(ring_copy(q, 1 - q % 2, half, 0))
+            start(ring_copy(q, 1 - half, half, 0))
 
     def lead_start(q):
-        way = q % 2
-        if q < 2:
-            far_block(way).wait_recv()
-        product = jnp.dot(far_w[way], lines(1, q), preferred_element_type=jnp.float32)
-        for half in range(2):
-            part[q, target(way, 3), half] += product[:, half * width:(half + 1) * width]
-            start(ring_copy(q, way, half, 0))
+        both = lines(1, q)
+        for half in range(2):
+            if q == 0:
+                far_block(half).wait_recv()
+            product = jnp.dot(
+                far_w[half], both[:, half * width:(half + 1) * width], preferred_element_type=jnp.float32
+            )
+            part[q, target(half, 3), half] += product
+            start(ring_copy(q, half, half, 0))
 
     def ring_step(q, lead, step):
-        way = q % 2 if lead else 1 - q % 2
-        for half in range(2):
+        for half in range(2):
+            way = half if lead else 1 - half
             ring_copy(q, way, half, step).wait_recv()
             if step < 2:
                 part[q, target(way, 2 - step), half] += arrived[q, way, step, half]
@@ -173,23 +184,23 @@
 
     own(0)
     own(1)
+    far(0)
+    near(0)
     own(2)
-    near(0)
+    far(1)
+    ring_start(0)
+    near(1)
     own(3)
-    near(1)
+    far(2)
+    ring_start(1)
     near(2)
-    far(0)
     own(0, 1)
     own(1, 1)
+    far(3)
+    ring_start(2)
     near(3)
     own(2, 1)
     own(3, 1)
-    ring_start(0)
-    far(1)
-    far(2)
-    ring_start(1)
-    far(3)
-    ring_start(2)
     ring_start(3)
     near(0, 1)
     near(1, 1)
@@ -212,13 +223,18 @@
     ring_step(3, False, 1)
     lead_start(2)
     lead_start(3)
+    weight_grad(1)
+    ring_step(0, True, 0)
+    ring_step(1, True, 0)
+    weight_grad(2)
+    ring_step(2, True, 0)
+    ring_step(3, True, 0)
+    weight_grad(3)
     for q in range(CHUNKS):
-        if q > 0:
-            weight_grad(q)
+        ring_step(q, True, 1)
+    for q in range(CHUNKS):
         ring_step(q, False, 2)
-    for step in range(3):
-        for q in range(CHUNKS):
-            ring_step(q, True, step)
+        ring_step(q, True, 2)
     for copy in pending:
         copy.wait_send()
 

time: 61.2 us -> 59 us (0.964)
  Pallas kernels: 58.3 us -> 56.6 us
    pallas_call x1, Pallas kernels: 58.3 us -> 56.6 us  [on_device(): pl.pallas_call(functools.partial(kernel, chips_z), out_shape=(pltpu.VMEM(...]
where the time goes in v3:
time: 59 us; the launch traced here: 58.9 us
  Pallas kernels  56.6 us (96%)
  local copies, waits for them, and re-layouts  1.69 us (3%)
  between operations  0.64 us (1%)
    pallas_call x1, Pallas kernels, on_device(): pl.pallas_call(functools.partial(kernel, chips_z), out_shape=(pltpu.VMEM(...  56.6 us
    unnamed x2, local copies, waits for them, and re-layouts  1.69 us

profile of v3, /device:TPU:1, one launch (start us, length us, event | category | flops | bytes accessed | tf_op | source)
XLA Modules:
  0.0 58.9 jit_solution(2129983962901540667)
XLA Ops:
  0.6 56.6 %shard_map.50 = (bf16[1,96,1024]{2,1,0:T(8,128)(2,1)S(1)}, bf16[1,768,768]{2,1,0:T(8,128)(2,1)S(1)}) custom-call(bf16[1,192,512]{2,1,0:T(8,128)(2,1)} %up.1, bf16[1,768,1024]{2,1,0:T(8,128)(2,1)} %attended.1, bf16[1,768,768]{2,1,0:T(8,128)(2,1)} %weight.1), custom_call_target="tpu_custom_call" | custom-call | tf_op jit(solution)/shard_map/pallas_call | solution.py:250
  57.2 0.7 %copy.7 = bf16[1,96,1024]{2,1,0:T(8,128)(2,1)} copy(bf16[1,96,1024]{2,1,0:T(8,128)(2,1)S(1)} %get-tuple-element.2) | data formatting | bytes 393216
  57.9 1.0 %copy.8 = bf16[1,768,768]{2,1,0:T(8,128)(2,1)} copy(bf16[1,768,768]{2,1,0:T(8,128)(2,1)S(1)} %get-tuple-element.3) | data formatting | bytes 2359296

commit v4 on v3

--- a/solution.py
+++ b/solution.py
@@ -239,6 +239,17 @@
         copy.wait_send()
 
 
+def write_out(ag, wg, ag_out, wg_out, sems):
+    copies = [
+        pltpu.make_async_copy(wg, wg_out, sems.at[0]),
+        pltpu.make_async_copy(ag, ag_out, sems.at[1]),
+    ]
+    for copy in copies:
+        copy.start()
+    for copy in copies:
+        copy.wait()
+
+
 def on_device(chips_z, upstream, attended, weight):
     _, lines, tokens = upstream.shape
     _, features, all_tokens = attended.shape
@@ -247,7 +258,7 @@
     width = tokens // CHUNKS
     bf16 = jnp.bfloat16
     dma = pltpu.SemaphoreType.DMA
-    return pl.pallas_call(
+    results = pl.pallas_call(
         functools.partial(kernel, chips_z),
         out_shape=(
             pltpu.VMEM((1, share, all_tokens), bf16),
@@ -273,6 +284,16 @@
         ],
         compiler_params=pltpu.CompilerParams(collective_id=0, has_side_effects=True),
     )(upstream, attended, weight)
+    return pl.pallas_call(
+        write_out,
+        out_shape=(
+            jax.ShapeDtypeStruct((1, share, all_tokens), bf16),
+            jax.ShapeDtypeStruct((1, rows, features), bf16),
+        ),
+        in_specs=[pl.BlockSpec(memory_space=pltpu.VMEM)] * 2,
+        out_specs=[pl.BlockSpec(memory_space=pl.ANY)] * 2,
+        scratch_shapes=[dma((2,))],
+    )(*[pltpu.with_memory_space_constraint(result, pltpu.VMEM) for result in results])
 
 
 def solution(mesh):

time: 59 us -> 58.4 us (0.990)
  local copies, waits for them, and re-layouts: 1.69 us -> 0 us
  Pallas kernels: 56.6 us -> 57.7 us
    unnamed x2 -> x0, local copies, waits for them, and re-layouts: 1.69 us -> none
    pallas_call x0 -> x1, Pallas kernels: none -> 1.08 us  [on_device(): pl.pallas_call(write_out, out_shape=(jax.ShapeDtypeStruct((1, share, all_...]
where the time goes in v4:
time: 58.4 us; the launch traced here: 58.3 us
  Pallas kernels  57.7 us (99%)
  between operations  0.64 us (1%)
    pallas_call x1, Pallas kernels, on_device(): pl.pallas_call(functools.partial(kernel, chips_z), out_shape=(pltpu.VMEM(...  56.6 us

profile of v4, /device:TPU:1, one launch (start us, length us, event | category | flops | bytes accessed | tf_op | source)
XLA Modules:
  0.0 58.3 jit_solution(18136882283696932577)
XLA Ops:
  0.6 56.6 %shard_map.50 = (bf16[1,96,1024]{2,1,0:T(8,128)(2,1)S(1)}, bf16[1,768,768]{2,1,0:T(8,128)(2,1)S(1)}) custom-call(bf16[1,192,512]{2,1,0:T(8,128)(2,1)} %up.1, bf16[1,768,1024]{2,1,0:T(8,128)(2,1)} %attended.1, bf16[1,768,768]{2,1,0:T(8,128)(2,1)} %weight.1), custom_call_target="tpu_custom_call" | custom-call | tf_op jit(solution)/shard_map/pallas_call | solution.py:261
  57.2 1.1 %shard_map.51 = (bf16[1,96,1024]{2,1,0:T(8,128)(2,1)}, bf16[1,768,768]{2,1,0:T(8,128)(2,1)}) custom-call(bf16[1,96,1024]{2,1,0:T(8,128)(2,1)S(1)} %get-tuple-element.4.ag, bf16[1,768,768]{2,1,0:T(8,128)(2,1)S(1)} %get-tuple-element.5.wg), custom_call_target="tpu_custom_call" | custom-call | tf_op jit(solution)/shard_map/pallas_call | solution.py:287
